TPU v7x, 256 devices: a whole 4x4x8 slice. The times are simulated.
256 devices in a mesh: seg: 8 (over y, core), ep: 32 (over z, x).
Axes of the slice: x: 4, y: 4, z: 8, core: 2. Of those that a mesh axis runs over, the one named last changes fastest.
Arguments:
- queries: bfloat16 [16384, 8192], P(('seg', 'ep')), may hold values from -6 to 6
- keys: bfloat16 [16384, 8192], P(('seg', 'ep')), may hold values from -1.25 to 1.25
- values: bfloat16 [16384, 8192], P(('seg', 'ep')), may hold values from -54 to 54
- log_decay: float32 [16384, 64], P('seg', 'ep'), may hold values from -1 to 0
- out_gain: float32 [8192], replicated, may hold values from 0.1 to 1.9
- out_proj: bfloat16 [8192, 6144], P('ep', 'seg'), may hold values from -0.0625 to 0.0625
- experts: int32 [2048, 2], P(('seg', 'ep')), may hold values from 0 to 15, all different within a row; in each aligned block of 8 rows (0 to 7, 8 to 15, ...) at most 2 rows name the same one
- gates: float32 [2048, 2], P(('seg', 'ep')), may hold values from 0.2 to 1
- up_weight: bfloat16 [32, 6144, 2304], P('ep', None, 'seg'), may hold values from -0.078125 to 0.078125
- down_weight: bfloat16 [32, 2304, 6144], P('ep', 'seg'), may hold values from -0.09375 to 0.09375
Outputs:
- attn_out: bfloat16 [16384, 8192], P(('seg', 'ep'))
- moe_out: bfloat16 [2048, 6144], P(('seg', 'ep'))
Inputs may be any that keep to these rules, and one draw needn't show every extreme that they name: Each row names two different experts. The 8 rows of one device name any one expert at most 2 times, and in some devices one expert exactly 2 times.
All inputs are finite; a program needn't handle non-finite values.
Results may differ from a plain program's by a relative error of at most 0.025.
Values may be sent and summed in bfloat16 or wider, within the bound.
No kernel may reach another device: no remote copies, remote signals or barrier semaphores. Data moves between devices by JAX's collectives and lax.ppermute only.
A program may use at most 128 MiB of HBM per device.

v0:
```python
import math
import jax
import jax.numpy as jnp
from jax import lax
from jax.sharding import Mesh
from jax.sharding import PartitionSpec as P

EP = ("ep_0", "ep_1")
SEG_EP = ("seg", "ep_0", "ep_1")
epsilon = 1e-06


def side_by_side(arrays, axis, dim, along):
    columns = [a.reshape(*a.shape[:along], -1) for a in arrays]
    both = jnp.concatenate(columns, axis=along)
    whole, at, done = (lax.all_gather(both, axis, axis=dim, tiled=True), 0, [])
    for a, column in zip(arrays, columns):
        section = whole[..., at : at + column.shape[along]]
        done.append(section.reshape(*section.shape[:along], *a.shape[along:]))
        at += column.shape[along]
    return tuple(done)


def sent_to_all(x, axis):
    devices = lax.axis_size(axis)
    return lax.all_to_all(jnp.broadcast_to(x[None], (devices, *x.shape)), axis, 0, 0, tiled=True)


def taken_together(x, axis):
    return sent_to_all(x, axis).sum(axis=0)


def scatter_axes(x, axes, dim):
    for axis in axes:
        x = lax.psum_scatter(x, axis, scatter_dimension=dim, tiled=True)
    return x


def route_tables(experts, gates, expert_count, capacity):
    token_count = experts.shape[0]
    flattened = experts.reshape(-1)
    onehot = (flattened[:, None] == jnp.arange(expert_count, dtype=jnp.int32)[None, :]).astype(
        jnp.int32
    )
    earlier = jnp.cumsum(onehot, axis=0) - onehot
    position = jnp.sum(earlier * onehot, axis=1)
    slot_index = (flattened * capacity + position).reshape(token_count, 2)
    columns = jnp.arange(expert_count * capacity, dtype=jnp.int32)
    matches = slot_index[:, :, None] == columns[None, None, :]
    dispatch = jnp.any(matches, axis=1).T.astype(jnp.bfloat16)
    combine = jnp.sum(jnp.where(matches, gates[:, :, None], 0.0), axis=1)
    return (dispatch, combine)


def expert_output(row_data, up_piece, down_piece):
    hidden = jax.nn.silu(jnp.dot(row_data, up_piece, preferred_element_type=jnp.float32)).astype(
        jnp.bfloat16
    )
    return jnp.dot(hidden, down_piece, preferred_element_type=jnp.float32)


def on_device(
    queries, keys, values, log_decay, out_gain, out_proj, experts, gates, up_weight, down_weight
):
    ep_count = lax.axis_size(EP)
    heads_local = log_decay.shape[1]
    head_dim = queries.shape[1] // (heads_local * ep_count)
    query_heads, key_heads, value_heads = (
        lax.all_to_all(queries, EP, split_axis=1, concat_axis=0, tiled=True),
        lax.all_to_all(keys, EP, split_axis=1, concat_axis=0, tiled=True),
        lax.all_to_all(values, EP, split_axis=1, concat_axis=0, tiled=True),
    )
    seg_length = query_heads.shape[0]
    query_heads = query_heads.reshape(seg_length, heads_local, head_dim)
    key_heads = key_heads.reshape(seg_length, heads_local, head_dim)
    value_heads = value_heads.reshape(seg_length, heads_local, head_dim)
    cumulative = jnp.cumsum(log_decay, axis=0)
    across = cumulative.T
    block_size = math.gcd(seg_length, 512)
    starts = jnp.arange(seg_length // block_size, dtype=jnp.int32) * block_size
    token_positions = jnp.arange(seg_length, dtype=jnp.int32)

    def block_mix(start):
        query_block = lax.dynamic_slice_in_dim(query_heads, start, block_size, 0)
        cum_block = lax.dynamic_slice_in_dim(across, start, block_size, 1)
        row_ids = start + jnp.arange(block_size, dtype=jnp.int32)
        causal = (row_ids[:, None] >= token_positions[None, :])[None]
        log_gap = cum_block[:, :, None] - across[:, None, :]
        weight = jnp.where(causal, jnp.exp(jnp.where(causal, log_gap, 0.0)), 0.0)
        scores = jnp.einsum(
            "thd,shd->hts", query_block, key_heads, preferred_element_type=jnp.float32
        )
        mixing = (scores * weight).astype(jnp.bfloat16)
        return jnp.einsum("hts,she->the", mixing, value_heads, preferred_element_type=jnp.float32)

    inside = lax.map(block_mix, starts).reshape(seg_length, heads_local, head_dim)
    ending = cumulative[-1]
    to_end = jnp.exp(ending[None, :] - cumulative)
    key_float = key_heads.astype(jnp.float32)
    value_float = value_heads.astype(jnp.float32)
    local_state = jnp.einsum("sh,shd,she->hde", to_end, key_float, value_float)
    all_ends, all_states = tuple(
        (
            part.astype(jnp.float32)
            for part in side_by_side(
                (ending[None].astype(jnp.bfloat16), local_state[None].astype(jnp.bfloat16)),
                "seg",
                0,
                2,
            )
        )
    )
    own_group = lax.axis_index("seg")
    group_ids = jnp.arange(all_ends.shape[0], dtype=jnp.int32)
    before = (group_ids < own_group)[:, None]
    through = jnp.cumsum(all_ends, axis=0)
    reaching = jnp.sum(jnp.where(before, all_ends, 0.0), axis=0)
    factors = jnp.where(before, jnp.exp(jnp.where(before, reaching[None, :] - through, 0.0)), 0.0)
    carried = jnp.einsum("gh,ghde->hde", factors, all_states)
    outside = jnp.exp(cumulative)[:, :, None] * jnp.einsum(
        "thd,hde->the", query_heads.astype(jnp.float32), carried
    )
    mixture = (inside + outside).astype(jnp.bfloat16).reshape(seg_length, heads_local * head_dim)
    token_mix = lax.all_to_all(mixture, EP, split_axis=0, concat_axis=1, tiled=True)
    as_float = token_mix.astype(jnp.float32)
    inv_rms = lax.rsqrt(jnp.mean(as_float * as_float, axis=1, keepdims=True) + epsilon)
    attn_out = (as_float * inv_rms * out_gain[None, :]).astype(jnp.bfloat16)
    row_stride = 8
    own_width = heads_local * head_dim
    feature_count = own_width * ep_count
    picked_float = mixture.reshape(seg_length // row_stride, row_stride, own_width)[:, 0].astype(
        jnp.float32
    )
    square_sums = taken_together(jnp.sum(picked_float * picked_float, axis=1), EP)
    picked_rms = lax.rsqrt(square_sums[:, None] / feature_count + epsilon)
    gain_slice = lax.dynamic_slice_in_dim(out_gain, lax.axis_index(EP) * own_width, own_width, 0)
    normed_rows = (picked_float * picked_rms * gain_slice[None, :]).astype(jnp.bfloat16)
    proj_terms = jnp.dot(
        normed_rows,
        lax.all_gather(out_proj, "seg", axis=1, tiled=True),
        preferred_element_type=jnp.float32,
    )
    moe_in = (
        scatter_axes(proj_terms.astype(jnp.bfloat16), EP, 0)
        .astype(jnp.float32)
        .astype(jnp.bfloat16)
    )
    expert_count = ep_count // 2
    token_count, model_width = moe_in.shape
    capacity = max(2, 4 * token_count // expert_count)
    dispatch, combine = route_tables(experts, gates, expert_count, capacity)
    up_piece = up_weight[0]
    down_piece = down_weight[0]
    slot_rows = jnp.dot(dispatch, moe_in, preferred_element_type=jnp.float32).astype(jnp.bfloat16)
    outgoing = jnp.repeat(slot_rows.reshape(expert_count, capacity, model_width), 2, axis=0)
    arrived = lax.all_to_all(outgoing, EP, split_axis=0, concat_axis=0, tiled=True).reshape(
        ep_count * capacity, model_width
    )
    gathered = lax.all_gather(arrived, "seg", axis=0, tiled=True)
    owned_sums = lax.psum_scatter(
        expert_output(gathered, up_piece, down_piece).astype(jnp.bfloat16),
        "seg",
        scatter_dimension=0,
        tiled=True,
    ).astype(jnp.float32)
    returned_back = lax.all_to_all(
        owned_sums.reshape(ep_count, capacity, model_width).astype(jnp.bfloat16),
        EP,
        split_axis=0,
        concat_axis=0,
        tiled=True,
    ).astype(jnp.float32)
    paired = returned_back.reshape(expert_count, 2, capacity, model_width)
    halves = (paired[:, 0] + paired[:, 1]).reshape(expert_count * capacity, model_width)
    summed = jnp.dot(combine, halves)
    moe_out = summed.astype(jnp.bfloat16)
    return (attn_out, moe_out)


def solution(mesh):
    torus = Mesh(mesh.devices.reshape(mesh.shape["seg"], 8, 4), ("seg", "ep_0", "ep_1"))
    placed = (
        P(SEG_EP, None),
        P(SEG_EP, None),
        P(SEG_EP, None),
        P("seg", EP),
        P(),
        P(EP, "seg"),
        P(SEG_EP, None),
        P(SEG_EP, None),
        P(EP, None, "seg"),
        P(EP, "seg", None),
    )
    return jax.shard_map(
        on_device,
        mesh=torus,
        in_specs=placed,
        out_specs=(P(SEG_EP, None), P(SEG_EP, None)),
        check_vma=False,
    )
```

profile of v0, /device:TPU:2, one launch (start us, length us, event | category | flops | bytes accessed | tf_op | source)
XLA Modules:
  0.0 520.2 jit_solution(4376102759249833830)
XLA Ops:
  7.2 2.5 copy.199
  9.7 11.8 %all-to-all-start.1 = ((bf16[64,32,256]{2,0,1:T(8,128)(2,1)}), bf16[64,32,256]{2,0,1:T(8,128)(2,1)}, u32[]{:S(2)}, u32[]{:S(2)}) async-start(bf16[64,32,256]{2,0,1:T(8,128)(2,1)} %bitcast.112), calls=%async_computation.1 | async-start | bytes 2097152 | tf_op jit(solution)/shard_map/all_to_all | solution.py:70
  21.5 2.3 copy.198
  23.8 25.8 %all-to-all-done.1 = bf16[64,32,256]{2,0,1:T(8,128)(2,1)} async-done(((bf16[64,32,256]{2,0,1:T(8,128)(2,1)}), bf16[64,32,256]{2,0,1:T(8,128)(2,1)}, u32[]{:S(2)}, u32[]{:S(2)}) %all-to-all-start.1) | async-done | bytes 1048608 | tf_op jit(solution)/shard_map/all_to_all | solution.py:70
  49.6 5.6 %all-to-all-start.2 = ((bf16[64,32,256]{2,0,1:T(8,128)(2,1)}), bf16[64,32,256]{2,0,1:T(8,128)(2,1)}, u32[]{:S(2)}, u32[]{:S(2)}) async-start(bf16[64,32,256]{2,0,1:T(8,128)(2,1)} %bitcast.110), calls=%async_computation.2 | async-start | bytes 2097152 | tf_op jit(solution)/shard_map/all_to_all | solution.py:71
  64.1 2.3 copy.200
  67.8 2.2 reshape.156
  70.0 12.2 %all-to-all-done.2 = bf16[64,32,256]{2,0,1:T(8,128)(2,1)} async-done(((bf16[64,32,256]{2,0,1:T(8,128)(2,1)}), bf16[64,32,256]{2,0,1:T(8,128)(2,1)}, u32[]{:S(2)}, u32[]{:S(2)}) %all-to-all-start.2) | async-done | bytes 1048608 | tf_op jit(solution)/shard_map/all_to_all | solution.py:71
  82.3 5.6 %all-to-all-start = ((bf16[64,32,256]{2,0,1:T(8,128)(2,1)}), bf16[64,32,256]{2,0,1:T(8,128)(2,1)}, u32[]{:S(2)}, u32[]{:S(2)}) async-start(bf16[64,32,256]{2,0,1:T(8,128)(2,1)} %bitcast.111), calls=%async_computation | async-start | bytes 2097152 | tf_op jit(solution)/shard_map/all_to_all | solution.py:69
  87.9 2.2 reshape.159
  90.1 5.6 %convert_multiply_fusion.1 = bf16[2048,2,128]{2,1,0:T(2,128)(2,1)S(1)} fusion(bf16[2048,2,128]{2,1,0:T(2,128)(2,1)} %reshape.156, f32[2048,2]{1,0:T(8,128)} %copy.139), kind=kLoop, calls=%fused_computation.27 | loop fusion | flops 1572864 | bytes 2113536 | tf_op jit(solution)/shard_map/sh,shd,she->hde/dot_general | solution.py:101
  95.7 2.5 fusion.18
  100.7 13.8 %all_gather.9 = bf16[8,2,16385]{2,1,0:T(2,128)(2,1)S(1)} all-gather(bf16[1,2,16385]{2,1,0:T(2,128)(2,1)S(1)} %pad_maximum_fusion), channel_id=1, replica_groups=mesh['seg'=8,'ep_0'=8,'ep_1'=4] {'seg'}, dimensions={0}, use_global_device_ids=true | all-gather | bytes 589860 | tf_op jit(solution)/shard_map/all_gather | solution.py:16
  116.0 2.4 copy.136
  120.3 2.2 reshape.163
  122.6 2.1 reshape.155
  124.7 2.3 copy.135
  127.0 99.5 %while.11 = (s32[]{:T(128)}, f32[4,512,2,128]{1,0,3,2:T(4,128)}, s32[4]{0:T(128)S(1)}, bf16[2048,2,128]{2,0,1:T(8,128)(2,1)}, bf16[2048,2,128]{2,0,1:T(8,128)(2,...) while((s32[]{:T(128)}, f32[4,512,2,128]{1,0,3,2:T(4,128)}, ...), condition=%wide.region_3.4_spmd.clone, body=%wide.region_2.3_spmd.clone.sunk | while | flops 1085276672 | bytes 7110819 | solution.py:96
  132.3 6.6 %fusion.58 = f32[1,512,2,128]{3,1,2,0:T(8,128)} fusion(bf16[2048,2,128]{2,0,1:T(8,128)(2,1)} %get-tuple-element.204, bf16[2048,2,128]{2,0,1:T(8,128)(2,1)} %get-tuple-element.202, f32[2,2048]{1,0:T(2,128)} %get-tuple-element.203, f32[2,512]{1,0:T(2,128)S(1)} %constant_dynamic-slice_fusion.2, pred[512,2048]{1,0:T(8,128)(4,1)} %iota_compare_fusion.5, ...), kind=kOutput, calls=%fused_computation.4.clone.1 | convolution fusion | flops 1084227584 | bytes 3952644 | tf_op jit(solution)/shard_map/while/body/eval_jaxpr/hts,she->the/dot_general | solution.py:94
  140.8 11.1 %dynamic_update_slice.6 = f32[4,512,2,128]{1,0,3,2:T(4,128)} dynamic-update-slice(f32[4,512,2,128]{1,0,3,2:T(4,128)} %get-tuple-element.189, f32[1,512,2,128]{1,0,3,2:T(1,128)} %copy.204, s32[]{:T(128)} %get-tuple-element.188, s32[]{:T(128)} %constant.22.clone.1..sunk, s32[]{:T(128)} %constant.22.clone.1..sunk, s32[]{:T(128)} %constant.22.clone.1..sunk) | dynamic-update-slice | bytes 1048580 | tf_op jit(solution)/shard_map/while/body/jit(dynamic_update_index_in_dim)/dynamic_update_slice | solution.py:96
  157.2 6.6 %fusion.58 = f32[1,512,2,128]{3,1,2,0:T(8,128)} fusion(bf16[2048,2,128]{2,0,1:T(8,128)(2,1)} %get-tuple-element.204, bf16[2048,2,128]{2,0,1:T(8,128)(2,1)} %get-tuple-element.202, f32[2,2048]{1,0:T(2,128)} %get-tuple-element.203, f32[2,512]{1,0:T(2,128)S(1)} %constant_dynamic-slice_fusion.2, pred[512,2048]{1,0:T(8,128)(4,1)} %iota_compare_fusion.5, ...), kind=kOutput, calls=%fused_computation.4.clone.1 | convolution fusion | flops 1084227584 | bytes 3952644 | tf_op jit(solution)/shard_map/while/body/eval_jaxpr/hts,she->the/dot_general | solution.py:94
  165.7 11.1 %dynamic_update_slice.6 = f32[4,512,2,128]{1,0,3,2:T(4,128)} dynamic-update-slice(f32[4,512,2,128]{1,0,3,2:T(4,128)} %get-tuple-element.189, f32[1,512,2,128]{1,0,3,2:T(1,128)} %copy.204, s32[]{:T(128)} %get-tuple-element.188, s32[]{:T(128)} %constant.22.clone.1..sunk, s32[]{:T(128)} %constant.22.clone.1..sunk, s32[]{:T(128)} %constant.22.clone.1..sunk) | dynamic-update-slice | bytes 1048580 | tf_op jit(solution)/shard_map/while/body/jit(dynamic_update_index_in_dim)/dynamic_update_slice | solution.py:96
  182.0 6.6 %fusion.58 = f32[1,512,2,128]{3,1,2,0:T(8,128)} fusion(bf16[2048,2,128]{2,0,1:T(8,128)(2,1)} %get-tuple-element.204, bf16[2048,2,128]{2,0,1:T(8,128)(2,1)} %get-tuple-element.202, f32[2,2048]{1,0:T(2,128)} %get-tuple-element.203, f32[2,512]{1,0:T(2,128)S(1)} %constant_dynamic-slice_fusion.2, pred[512,2048]{1,0:T(8,128)(4,1)} %iota_compare_fusion.5, ...), kind=kOutput, calls=%fused_computation.4.clone.1 | convolution fusion | flops 1084227584 | bytes 3952644 | tf_op jit(solution)/shard_map/while/body/eval_jaxpr/hts,she->the/dot_general | solution.py:94
  190.5 11.1 %dynamic_update_slice.6 = f32[4,512,2,128]{1,0,3,2:T(4,128)} dynamic-update-slice(f32[4,512,2,128]{1,0,3,2:T(4,128)} %get-tuple-element.189, f32[1,512,2,128]{1,0,3,2:T(1,128)} %copy.204, s32[]{:T(128)} %get-tuple-element.188, s32[]{:T(128)} %constant.22.clone.1..sunk, s32[]{:T(128)} %constant.22.clone.1..sunk, s32[]{:T(128)} %constant.22.clone.1..sunk) | dynamic-update-slice | bytes 1048580 | tf_op jit(solution)/shard_map/while/body/jit(dynamic_update_index_in_dim)/dynamic_update_slice | solution.py:96
  206.9 6.6 %fusion.58 = f32[1,512,2,128]{3,1,2,0:T(8,128)} fusion(bf16[2048,2,128]{2,0,1:T(8,128)(2,1)} %get-tuple-element.204, bf16[2048,2,128]{2,0,1:T(8,128)(2,1)} %get-tuple-element.202, f32[2,2048]{1,0:T(2,128)} %get-tuple-element.203, f32[2,512]{1,0:T(2,128)S(1)} %constant_dynamic-slice_fusion.2, pred[512,2048]{1,0:T(8,128)(4,1)} %iota_compare_fusion.5, ...), kind=kOutput, calls=%fused_computation.4.clone.1 | convolution fusion | flops 1084227584 | bytes 3952644 | tf_op jit(solution)/shard_map/while/body/eval_jaxpr/hts,she->the/dot_general | solution.py:94
  215.4 11.1 %dynamic_update_slice.6 = f32[4,512,2,128]{1,0,3,2:T(4,128)} dynamic-update-slice(f32[4,512,2,128]{1,0,3,2:T(4,128)} %get-tuple-element.189, f32[1,512,2,128]{1,0,3,2:T(1,128)} %copy.204, s32[]{:T(128)} %get-tuple-element.188, s32[]{:T(128)} %constant.22.clone.1..sunk, s32[]{:T(128)} %constant.22.clone.1..sunk, s32[]{:T(128)} %constant.22.clone.1..sunk) | dynamic-update-slice | bytes 1048580 | tf_op jit(solution)/shard_map/while/body/jit(dynamic_update_index_in_dim)/dynamic_update_slice | solution.py:96
  226.5 3.7 reshape.160
  233.2 3.4 fusion.14
  236.6 3.7 copy.145
  240.3 2.5 reshape_reshape.3
  245.6 9.8 %all-to-all-start.4 = ((f32[32,1,256]{2,1,0:T(1,128)}), f32[32,1,256]{2,1,0:T(1,128)}, u32[]{:S(2)}, u32[]{:S(2)}) async-start(f32[32,1,256]{2,1,0:T(1,128)} %broadcast_in_dim.85), calls=%async_computation.4 | async-start | bytes 65536 | tf_op jit(solution)/shard_map/all_to_all | solution.py:26
  256.3 7.8 %all-to-all-done.4 = f32[32,1,256]{2,1,0:T(1,128)} async-done(((f32[32,1,256]{2,1,0:T(1,128)}), f32[32,1,256]{2,1,0:T(1,128)}, u32[]{:S(2)}, u32[]{:S(2)}) %all-to-all-start.4) | async-done | bytes 32800 | tf_op jit(solution)/shard_map/all_to_all | solution.py:26
  265.0 4.7 convolution_convert_fusion.1
  269.8 41.9 %reduce-scatter.4.cloned.1.call-done = bf16[32,6144]{1,0:T(8,128)(2,1)} async-done(((bf16[256,6144]{1,0:T(8,128)(2,1)}), bf16[32,6144]{1,0:T(8,128)(2,1)}) %reduce-scatter.4.cloned.1.call-update) | async-done | bytes 393232 | tf_op jit(solution)/shard_map/reduce_scatter | solution.py:35
  315.2 19.9 %reduce-scatter.6.cloned.1.call-done = bf16[8,6144]{1,0:T(8,128)(2,1)} async-done(((bf16[32,6144]{1,0:T(8,128)(2,1)}), bf16[8,6144]{1,0:T(8,128)(2,1)}) %reduce-scatter.6.cloned.1.call-update) | async-done | bytes 98320 | tf_op jit(solution)/shard_map/reduce_scatter | solution.py:35
  337.0 2.0 reshape.164
  340.4 30.7 %all_to_all.77 = bf16[32,2,6144]{2,1,0:T(2,128)(2,1)} all-to-all(bf16[32,2,6144]{2,1,0:T(2,128)(2,1)S(1)} %bitcast.113), channel_id=1, replica_groups=mesh['seg'=8,'ep_0'=8,'ep_1'=4] {'ep_0','ep_1'}, dimensions={0} | all-to-all | bytes 1572864 | tf_op jit(solution)/shard_map/all_to_all | solution.py:156
  371.2 3.0 reshape.166
  374.2 40.3 %all-gather.5.cloned.1.call-done = bf16[512,6144]{1,0:T(8,128)(2,1)} async-done(((bf16[64,6144]{1,0:T(8,128)(2,1)}), bf16[512,6144]{1,0:T(8,128)(2,1)}) %all-gather.5.cloned.1.call-update) | async-done | bytes 6291472 | tf_op jit(solution)/shard_map/all_gather | solution.py:159
  414.5 12.0 %convolution_convert_fusion = bf16[512,6144]{1,0:T(8,128)(2,1)} fusion(bf16[1,288,6144]{2,1,0:T(8,128)(2,1)S(1)} %copy-done, bf16[512,6144]{1,0:T(8,128)(2,1)} %all-gather.5.cloned.1.call-done, bf16[1,6144,288]{1,2,0:T(8,128)(2,1)} %param.20), kind=kOutput, calls=%fused_computation.10 | convolution fusion | flops 3627761664 | bytes 19660800 | tf_op jit(solution)/shard_map/dot_general | solution.py:59
  426.6 2.5 all_to_all.65
  429.1 10.2 %all-to-all-start.3 = ((bf16[32,64,256]{2,1,0:T(8,128)(2,1)}), bf16[32,64,256]{2,1,0:T(8,128)(2,1)}, u32[]{:S(2)}, u32[]{:S(2)}) async-start(bf16[32,64,256]{2,1,0:T(8,128)(2,1)} %all_to_all.65), calls=%async_computation.3 | async-start | bytes 2097152 | tf_op jit(solution)/shard_map/all_to_all | solution.py:124
  439.4 28.5 %all-to-all-done.3 = bf16[32,64,256]{2,1,0:T(8,128)(2,1)} async-done(((bf16[32,64,256]{2,1,0:T(8,128)(2,1)}), bf16[32,64,256]{2,1,0:T(8,128)(2,1)}, u32[]{:S(2)}, u32[]{:S(2)}) %all-to-all-start.3) | async-done | bytes 1048608 | tf_op jit(solution)/shard_map/all_to_all | solution.py:124
  472.5 2.9 convert_element_type.93
  475.3 9.8 %all-to-all-start.6 = ((bf16[32,2,6144]{2,1,0:T(2,128)(2,1)}), bf16[32,2,6144]{2,1,0:T(2,128)(2,1)}, u32[]{:S(2)}, u32[]{:S(2)}) async-start(bf16[32,2,6144]{2,1,0:T(2,128)(2,1)} %convert_element_type.93), calls=%async_computation.9 | async-start | bytes 1572864 | tf_op jit(solution)/shard_map/all_to_all | solution.py:166
  485.2 2.8 multiply_convert_fusion.1
  488.0 18.8 %all-to-all-done.6 = bf16[32,2,6144]{2,1,0:T(2,128)(2,1)} async-done(((bf16[32,2,6144]{2,1,0:T(2,128)(2,1)}), bf16[32,2,6144]{2,1,0:T(2,128)(2,1)}, u32[]{:S(2)}, u32[]{:S(2)}) %all-to-all-start.6) | async-done | bytes 786464 | tf_op jit(solution)/shard_map/all_to_all | solution.py:166
  506.8 2.0 convert.7
  (98 shorter events, 62.2 us)
Async XLA Ops:
  7.2 407.3 %copy-start = (bf16[1,288,6144]{2,1,0:T(8,128)(2,1)S(1)}, bf16[1,288,6144]{2,1,0:T(8,128)(2,1)}, u32[]{:S(2)}) copy-start(bf16[1,288,6144]{2,1,0:T(8,128)(2,1)} %param.21) | copy-start | bytes 10616836
  9.7 46.3 %copy-start.4 = (f32[2048,2]{0,1:T(2,128)S(1)}, f32[2048,2]{0,1:T(2,128)}, u32[]{:S(2)}) copy-start(f32[2048,2]{0,1:T(2,128)} %param.15) | copy-start | bytes 49156
  9.7 39.9 %all-to-all-start.1 = ((bf16[64,32,256]{2,0,1:T(8,128)(2,1)}), bf16[64,32,256]{2,0,1:T(8,128)(2,1)}, u32[]{:S(2)}, u32[]{:S(2)}) async-start(bf16[64,32,256]{2,0,1:T(8,128)(2,1)} %bitcast.112), calls=%async_computation.1 | async-start | bytes 2097152 | tf_op jit(solution)/shard_map/all_to_all | solution.py:70
  49.6 32.7 %all-to-all-start.2 = ((bf16[64,32,256]{2,0,1:T(8,128)(2,1)}), bf16[64,32,256]{2,0,1:T(8,128)(2,1)}, u32[]{:S(2)}, u32[]{:S(2)}) async-start(bf16[64,32,256]{2,0,1:T(8,128)(2,1)} %bitcast.110), calls=%async_computation.2 | async-start | bytes 2097152 | tf_op jit(solution)/shard_map/all_to_all | solution.py:71
  55.2 209.8 %all-gather.3.cloned.1.call-start = ((), (), s32[]{:S(2)}) async-start(), calls=%async_computation.10 | async-start | bytes 3538944 | tf_op jit(solution)/shard_map/all_gather | solution.py:140
  82.3 40.3 %all-to-all-start = ((bf16[64,32,256]{2,0,1:T(8,128)(2,1)}), bf16[64,32,256]{2,0,1:T(8,128)(2,1)}, u32[]{:S(2)}, u32[]{:S(2)}) async-start(bf16[64,32,256]{2,0,1:T(8,128)(2,1)} %bitcast.111), calls=%async_computation | async-start | bytes 2097152 | tf_op jit(solution)/shard_map/all_to_all | solution.py:69
  99.6 18.7 %copy-start.1 = (bf16[2048,2,128]{2,1,0:T(2,128)(2,1)S(1)}, bf16[2048,2,128]{2,1,0:T(2,128)(2,1)}, u32[]{:S(2)}) copy-start(bf16[2048,2,128]{2,1,0:T(2,128)(2,1)} %reshape.159) | copy-start | bytes 3145732
  119.6 7.4 %copy-start.7 = (bf16[8,2,1]{0,1,2:T(2,128)(2,1)}, bf16[8,2,1]{0,1,2:T(2,128)(2,1)S(1)}, u32[]{:S(2)}) copy-start(bf16[8,2,1]{0,1,2:T(2,128)(2,1)S(1)} %copy.159) | copy-start | bytes 100
  226.5 6.7 %copy-start.3 = (f32[2048,2]{0,1:T(2,128)S(1)}, f32[2048,2]{0,1:T(2,128)}, u32[]{:S(2)}) copy-start(f32[2048,2]{0,1:T(2,128)} %get-tuple-element.131) | copy-start | bytes 49156
  244.2 0.7 copy-start.2
  245.6 18.5 %all-to-all-start.4 = ((f32[32,1,256]{2,1,0:T(1,128)}), f32[32,1,256]{2,1,0:T(1,128)}, u32[]{:S(2)}, u32[]{:S(2)}) async-start(f32[32,1,256]{2,1,0:T(1,128)} %broadcast_in_dim.85), calls=%async_computation.4 | async-start | bytes 65536 | tf_op jit(solution)/shard_map/all_to_all | solution.py:26
  255.5 56.2 %reduce-scatter.4.cloned.1.call-start = ((), (), s32[]{:S(2)}) async-start(), calls=%async_computation.11 | async-start | bytes 3538944 | tf_op jit(solution)/shard_map/reduce_scatter | solution.py:35
  269.7 42.3 %copy-start.5 = (s32[8,2]{0,1:T(2,128)S(1)}, s32[8,2]{0,1:T(2,128)}, u32[]{:S(2)}) copy-start(s32[8,2]{0,1:T(2,128)} %param.18) | copy-start | bytes 196
  269.7 65.3 %reduce-scatter.6.cloned.1.call-start = ((), (), s32[]{:S(2)}) async-start(), calls=%async_computation.12 | async-start | bytes 491520 | tf_op jit(solution)/shard_map/reduce_scatter | solution.py:35
  311.7 102.8 %all-gather.5.cloned.1.call-start = ((), (), s32[]{:S(2)}) async-start(), calls=%async_computation.13 | async-start | bytes 7077888 | tf_op jit(solution)/shard_map/all_gather | solution.py:159
  374.1 98.3 %reduce-scatter.8.cloned.1.call-start = ((), (), s32[]{:S(2)}) async-start(), calls=%async_computation.14 | async-start | bytes 7077888 | tf_op jit(solution)/shard_map/reduce_scatter | solution.py:160
  426.6 12.8 %copy-start.6 = (f32[8,2]{0,1:T(2,128)S(1)}, f32[8,2]{0,1:T(2,128)}, u32[]{:S(2)}) copy-start(f32[8,2]{0,1:T(2,128)} %param.19) | copy-start | bytes 196
  429.1 38.7 %all-to-all-start.3 = ((bf16[32,64,256]{2,1,0:T(8,128)(2,1)}), bf16[32,64,256]{2,1,0:T(8,128)(2,1)}, u32[]{:S(2)}, u32[]{:S(2)}) async-start(bf16[32,64,256]{2,1,0:T(8,128)(2,1)} %all_to_all.65), calls=%async_computation.3 | async-start | bytes 2097152 | tf_op jit(solution)/shard_map/all_to_all | solution.py:124
  475.3 31.5 %all-to-all-start.6 = ((bf16[32,2,6144]{2,1,0:T(2,128)(2,1)}), bf16[32,2,6144]{2,1,0:T(2,128)(2,1)}, u32[]{:S(2)}, u32[]{:S(2)}) async-start(bf16[32,2,6144]{2,1,0:T(2,128)(2,1)} %convert_element_type.93), calls=%async_computation.9 | async-start | bytes 1572864 | tf_op jit(solution)/shard_map/all_to_all | solution.py:166
Sparse Core Ops, SparseCore 0:
  57.9 31.4 all-gather.2
  269.8 41.8 reduce-scatter.3
  314.2 20.7 reduce-scatter.5
  374.2 40.2 all-gather.4
  426.7 45.5 reduce-scatter.7
where the time goes:
time: 524 us; the launch traced here: 520 us
  waiting for transfers between devices  196 us (37%)
  local copies, waits for them, and re-layouts  115 us (22%)
  matrix products  54.1 us (10%)
  starting transfers between devices  53.3 us (10%)
  blocking collectives  44.5 us (8%)
  other arithmetic  36.2 us (7%)
  between operations  14 us (3%)
  loops' own time  6.62 us (1%)
    reduce_scatter x2, waiting for transfers between devices, scatter_axes(): x = lax.psum_scatter(x, axis, scatter_dimension=dim, tiled=True)  61.8 us
    dynamic_update_slice x8, local copies, waits for them, and re-layouts, on_device(): lax.map(block_mix, starts).reshape(seg_length, heads_local, head_dim)  52.2 us
    all_gather x1, waiting for transfers between devices, on_device(): gathered = lax.all_gather(arrived, 'seg', axis=0, tiled=True)  40.3 us
    all_to_all x1, blocking collectives, on_device(): lax.all_to_all(outgoing, EP, split_axis=0, concat_axis=0, tiled=True)  30.7 us
    all_to_all x1, waiting for transfers between devices, on_device(): lax.all_to_all(mixture, EP, split_axis=0, concat_axis=1, tiled=True)  28.5 us
    dot_general x4, matrix products, block_mix(): jnp.einsum('hts,she->the', mixing, value_heads, preferred_element_type=jn...  26.3 us
    all_to_all x1, waiting for transfers between devices, on_device(): lax.all_to_all(keys, EP, split_axis=1, concat_axis=0, tiled=True)  25.8 us
    all_to_all x1, waiting for transfers between devices, on_device(): lax.all_to_all(owned_sums.reshape(ep_count, capacity, model_width).astype...  18.8 us
  transfers between devices with their start and end apart: 11, of which 8 were waited for; matrix products, arithmetic and copies ran while one was open for 32% of the time, Pallas kernels for 0%

commit v1 on v0

--- a/solution.py
+++ b/solution.py
@@ -156,7 +156,9 @@
     arrived = lax.all_to_all(outgoing, EP, split_axis=0, concat_axis=0, tiled=True).reshape(
         ep_count * capacity, model_width
     )
-    gathered = lax.all_gather(arrived, "seg", axis=0, tiled=True)
+    gathered = jnp.concatenate(
+        lax.all_to_all(jnp.stack([arrived] * lax.axis_size("seg")), "seg", 0, 0), axis=0
+    )
     owned_sums = lax.psum_scatter(
         expert_output(gathered, up_piece, down_piece).astype(jnp.bfloat16),
         "seg",

time: 524 us -> 557 us (1.063)
  blocking collectives: 44.5 us -> 122 us
  waiting for transfers between devices: 196 us -> 155 us
    all_to_all x0 -> x1, blocking collectives: none -> 77.4 us  [on_device(): lax.all_to_all(jnp.stack([arrived] * lax.axis_size('seg')), 'seg', 0, 0)]
    all_gather x1 -> x0, waiting for transfers between devices: 40.3 us -> none  [on_device(): gathered = lax.all_gather(arrived, 'seg', axis=0, tiled=True)]
  transfers between devices with their start and end apart: 11 -> 10, of which waited for: 8 -> 7; matrix products, arithmetic and copies ran while one was open for 32% -> 30% of each run, Pallas kernels for 0% -> 0%
where the time goes in v1:
time: 557 us; the launch traced here: 554 us
  waiting for transfers between devices  155 us (28%)
  blocking collectives  122 us (22%)
  local copies, waits for them, and re-layouts  117 us (21%)
  matrix products  54.1 us (10%)
  starting transfers between devices  48.9 us (9%)
  other arithmetic  36.2 us (6%)
  between operations  14 us (3%)
  loops' own time  6.62 us (1%)
    all_to_all x1, blocking collectives, on_device(): lax.all_to_all(jnp.stack([arrived] * lax.axis_size('seg')), 'seg', 0, 0)  77.4 us
    reduce_scatter x2, waiting for transfers between devices, scatter_axes(): x = lax.psum_scatter(x, axis, scatter_dimension=dim, tiled=True)  61.8 us
    dynamic_update_slice x8, local copies, waits for them, and re-layouts, on_device(): lax.map(block_mix, starts).reshape(seg_length, heads_local, head_dim)  52.2 us
    all_to_all x1, blocking collectives, on_device(): lax.all_to_all(outgoing, EP, split_axis=0, concat_axis=0, tiled=True)  30.7 us
    all_to_all x1, waiting for transfers between devices, on_device(): lax.all_to_all(mixture, EP, split_axis=0, concat_axis=1, tiled=True)  27.7 us
    dot_general x4, matrix products, block_mix(): jnp.einsum('hts,she->the', mixing, value_heads, preferred_element_type=jn...  26.3 us
    all_to_all x1, waiting for transfers between devices, on_device(): lax.all_to_all(keys, EP, split_axis=1, concat_axis=0, tiled=True)  25.8 us
    all_to_all x1, waiting for transfers between devices, on_device(): lax.all_to_all(owned_sums.reshape(ep_count, capacity, model_width).astype...  18.8 us
  transfers between devices with their start and end apart: 10, of which 7 were waited for; matrix products, arithmetic and copies ran while one was open for 30% of the time, Pallas kernels for 0%

profile of v1, /device:TPU:2, one launch (start us, length us, event | category | flops | bytes accessed | tf_op | source)
XLA Modules:
  0.0 553.8 jit_solution(17855462094516664908)
XLA Ops:
  7.2 2.5 copy.199
  9.7 11.8 %all-to-all-start.1 = ((bf16[64,32,256]{2,0,1:T(8,128)(2,1)}), bf16[64,32,256]{2,0,1:T(8,128)(2,1)}, u32[]{:S(2)}, u32[]{:S(2)}) async-start(bf16[64,32,256]{2,0,1:T(8,128)(2,1)} %bitcast.114), calls=%async_computation.1 | async-start | bytes 2097152 | tf_op jit(solution)/shard_map/all_to_all | solution.py:70
  21.5 2.3 copy.198
  23.8 25.8 %all-to-all-done.1 = bf16[64,32,256]{2,0,1:T(8,128)(2,1)} async-done(((bf16[64,32,256]{2,0,1:T(8,128)(2,1)}), bf16[64,32,256]{2,0,1:T(8,128)(2,1)}, u32[]{:S(2)}, u32[]{:S(2)}) %all-to-all-start.1) | async-done | bytes 1048608 | tf_op jit(solution)/shard_map/all_to_all | solution.py:70
  49.6 5.6 %all-to-all-start.2 = ((bf16[64,32,256]{2,0,1:T(8,128)(2,1)}), bf16[64,32,256]{2,0,1:T(8,128)(2,1)}, u32[]{:S(2)}, u32[]{:S(2)}) async-start(bf16[64,32,256]{2,0,1:T(8,128)(2,1)} %bitcast.112), calls=%async_computation.2 | async-start | bytes 2097152 | tf_op jit(solution)/shard_map/all_to_all | solution.py:71
  64.1 2.3 copy.200
  67.8 2.2 reshape.158
  70.0 12.2 %all-to-all-done.2 = bf16[64,32,256]{2,0,1:T(8,128)(2,1)} async-done(((bf16[64,32,256]{2,0,1:T(8,128)(2,1)}), bf16[64,32,256]{2,0,1:T(8,128)(2,1)}, u32[]{:S(2)}, u32[]{:S(2)}) %all-to-all-start.2) | async-done | bytes 1048608 | tf_op jit(solution)/shard_map/all_to_all | solution.py:71
  82.3 5.6 %all-to-all-start = ((bf16[64,32,256]{2,0,1:T(8,128)(2,1)}), bf16[64,32,256]{2,0,1:T(8,128)(2,1)}, u32[]{:S(2)}, u32[]{:S(2)}) async-start(bf16[64,32,256]{2,0,1:T(8,128)(2,1)} %bitcast.113), calls=%async_computation | async-start | bytes 2097152 | tf_op jit(solution)/shard_map/all_to_all | solution.py:69
  87.9 2.2 reshape.161
  90.1 5.6 %convert_multiply_fusion.1 = bf16[2048,2,128]{2,1,0:T(2,128)(2,1)S(1)} fusion(bf16[2048,2,128]{2,1,0:T(2,128)(2,1)} %reshape.158, f32[2048,2]{1,0:T(8,128)} %copy.139), kind=kLoop, calls=%fused_computation.27 | loop fusion | flops 1572864 | bytes 2113536 | tf_op jit(solution)/shard_map/sh,shd,she->hde/dot_general | solution.py:101
  95.7 2.5 fusion.18
  100.7 13.8 %all_gather.6 = bf16[8,2,16385]{2,1,0:T(2,128)(2,1)S(1)} all-gather(bf16[1,2,16385]{2,1,0:T(2,128)(2,1)S(1)} %pad_maximum_fusion), channel_id=1, replica_groups=mesh['seg'=8,'ep_0'=8,'ep_1'=4] {'seg'}, dimensions={0}, use_global_device_ids=true | all-gather | bytes 589860 | tf_op jit(solution)/shard_map/all_gather | solution.py:16
  116.0 2.4 copy.136
  120.3 2.2 reshape.165
  122.6 2.1 reshape.157
  124.7 2.3 copy.135
  127.0 99.5 %while.11 = (s32[]{:T(128)}, f32[4,512,2,128]{1,0,3,2:T(4,128)}, s32[4]{0:T(128)S(1)}, bf16[2048,2,128]{2,0,1:T(8,128)(2,1)}, bf16[2048,2,128]{2,0,1:T(8,128)(2,...) while((s32[]{:T(128)}, f32[4,512,2,128]{1,0,3,2:T(4,128)}, ...), condition=%wide.region_3.4_spmd.clone, body=%wide.region_2.3_spmd.clone.sunk | while | flops 1085276672 | bytes 7110819 | solution.py:96
  132.3 6.6 %fusion.58 = f32[1,512,2,128]{3,1,2,0:T(8,128)} fusion(bf16[2048,2,128]{2,0,1:T(8,128)(2,1)} %get-tuple-element.204, bf16[2048,2,128]{2,0,1:T(8,128)(2,1)} %get-tuple-element.202, f32[2,2048]{1,0:T(2,128)} %get-tuple-element.203, f32[2,512]{1,0:T(2,128)S(1)} %constant_dynamic-slice_fusion.2, pred[512,2048]{1,0:T(8,128)(4,1)} %iota_compare_fusion.5, ...), kind=kOutput, calls=%fused_computation.4.clone.1 | convolution fusion | flops 1084227584 | bytes 3952644 | tf_op jit(solution)/shard_map/while/body/eval_jaxpr/hts,she->the/dot_general | solution.py:94
  140.8 11.1 %dynamic_update_slice.6 = f32[4,512,2,128]{1,0,3,2:T(4,128)} dynamic-update-slice(f32[4,512,2,128]{1,0,3,2:T(4,128)} %get-tuple-element.189, f32[1,512,2,128]{1,0,3,2:T(1,128)} %copy.204, s32[]{:T(128)} %get-tuple-element.188, s32[]{:T(128)} %constant.22.clone.1..sunk, s32[]{:T(128)} %constant.22.clone.1..sunk, s32[]{:T(128)} %constant.22.clone.1..sunk) | dynamic-update-slice | bytes 1048580 | tf_op jit(solution)/shard_map/while/body/jit(dynamic_update_index_in_dim)/dynamic_update_slice | solution.py:96
  157.2 6.6 %fusion.58 = f32[1,512,2,128]{3,1,2,0:T(8,128)} fusion(bf16[2048,2,128]{2,0,1:T(8,128)(2,1)} %get-tuple-element.204, bf16[2048,2,128]{2,0,1:T(8,128)(2,1)} %get-tuple-element.202, f32[2,2048]{1,0:T(2,128)} %get-tuple-element.203, f32[2,512]{1,0:T(2,128)S(1)} %constant_dynamic-slice_fusion.2, pred[512,2048]{1,0:T(8,128)(4,1)} %iota_compare_fusion.5, ...), kind=kOutput, calls=%fused_computation.4.clone.1 | convolution fusion | flops 1084227584 | bytes 3952644 | tf_op jit(solution)/shard_map/while/body/eval_jaxpr/hts,she->the/dot_general | solution.py:94
  165.7 11.1 %dynamic_update_slice.6 = f32[4,512,2,128]{1,0,3,2:T(4,128)} dynamic-update-slice(f32[4,512,2,128]{1,0,3,2:T(4,128)} %get-tuple-element.189, f32[1,512,2,128]{1,0,3,2:T(1,128)} %copy.204, s32[]{:T(128)} %get-tuple-element.188, s32[]{:T(128)} %constant.22.clone.1..sunk, s32[]{:T(128)} %constant.22.clone.1..sunk, s32[]{:T(128)} %constant.22.clone.1..sunk) | dynamic-update-slice | bytes 1048580 | tf_op jit(solution)/shard_map/while/body/jit(dynamic_update_index_in_dim)/dynamic_update_slice | solution.py:96
  182.0 6.6 %fusion.58 = f32[1,512,2,128]{3,1,2,0:T(8,128)} fusion(bf16[2048,2,128]{2,0,1:T(8,128)(2,1)} %get-tuple-element.204, bf16[2048,2,128]{2,0,1:T(8,128)(2,1)} %get-tuple-element.202, f32[2,2048]{1,0:T(2,128)} %get-tuple-element.203, f32[2,512]{1,0:T(2,128)S(1)} %constant_dynamic-slice_fusion.2, pred[512,2048]{1,0:T(8,128)(4,1)} %iota_compare_fusion.5, ...), kind=kOutput, calls=%fused_computation.4.clone.1 | convolution fusion | flops 1084227584 | bytes 3952644 | tf_op jit(solution)/shard_map/while/body/eval_jaxpr/hts,she->the/dot_general | solution.py:94
  190.5 11.1 %dynamic_update_slice.6 = f32[4,512,2,128]{1,0,3,2:T(4,128)} dynamic-update-slice(f32[4,512,2,128]{1,0,3,2:T(4,128)} %get-tuple-element.189, f32[1,512,2,128]{1,0,3,2:T(1,128)} %copy.204, s32[]{:T(128)} %get-tuple-element.188, s32[]{:T(128)} %constant.22.clone.1..sunk, s32[]{:T(128)} %constant.22.clone.1..sunk, s32[]{:T(128)} %constant.22.clone.1..sunk) | dynamic-update-slice | bytes 1048580 | tf_op jit(solution)/shard_map/while/body/jit(dynamic_update_index_in_dim)/dynamic_update_slice | solution.py:96
  206.9 6.6 %fusion.58 = f32[1,512,2,128]{3,1,2,0:T(8,128)} fusion(bf16[2048,2,128]{2,0,1:T(8,128)(2,1)} %get-tuple-element.204, bf16[2048,2,128]{2,0,1:T(8,128)(2,1)} %get-tuple-element.202, f32[2,2048]{1,0:T(2,128)} %get-tuple-element.203, f32[2,512]{1,0:T(2,128)S(1)} %constant_dynamic-slice_fusion.2, pred[512,2048]{1,0:T(8,128)(4,1)} %iota_compare_fusion.5, ...), kind=kOutput, calls=%fused_computation.4.clone.1 | convolution fusion | flops 1084227584 | bytes 3952644 | tf_op jit(solution)/shard_map/while/body/eval_jaxpr/hts,she->the/dot_general | solution.py:94
  215.4 11.1 %dynamic_update_slice.6 = f32[4,512,2,128]{1,0,3,2:T(4,128)} dynamic-update-slice(f32[4,512,2,128]{1,0,3,2:T(4,128)} %get-tuple-element.189, f32[1,512,2,128]{1,0,3,2:T(1,128)} %copy.204, s32[]{:T(128)} %get-tuple-element.188, s32[]{:T(128)} %constant.22.clone.1..sunk, s32[]{:T(128)} %constant.22.clone.1..sunk, s32[]{:T(128)} %constant.22.clone.1..sunk) | dynamic-update-slice | bytes 1048580 | tf_op jit(solution)/shard_map/while/body/jit(dynamic_update_index_in_dim)/dynamic_update_slice | solution.py:96
  226.5 3.7 reshape.162
  233.2 3.4 fusion.14
  236.6 3.7 copy.145
  240.3 2.5 reshape_reshape.3
  245.6 9.8 %all-to-all-start.4 = ((f32[32,1,256]{2,1,0:T(1,128)}), f32[32,1,256]{2,1,0:T(1,128)}, u32[]{:S(2)}, u32[]{:S(2)}) async-start(f32[32,1,256]{2,1,0:T(1,128)} %broadcast_in_dim.85), calls=%async_computation.4 | async-start | bytes 65536 | tf_op jit(solution)/shard_map/all_to_all | solution.py:26
  256.3 7.8 %all-to-all-done.4 = f32[32,1,256]{2,1,0:T(1,128)} async-done(((f32[32,1,256]{2,1,0:T(1,128)}), f32[32,1,256]{2,1,0:T(1,128)}, u32[]{:S(2)}, u32[]{:S(2)}) %all-to-all-start.4) | async-done | bytes 32800 | tf_op jit(solution)/shard_map/all_to_all | solution.py:26
  265.0 4.7 convolution_convert_fusion.1
  269.8 41.9 %reduce-scatter.4.cloned.1.call-done = bf16[32,6144]{1,0:T(8,128)(2,1)} async-done(((bf16[256,6144]{1,0:T(8,128)(2,1)}), bf16[32,6144]{1,0:T(8,128)(2,1)}) %reduce-scatter.4.cloned.1.call-update) | async-done | bytes 393232 | tf_op jit(solution)/shard_map/reduce_scatter | solution.py:35
  315.2 19.9 %reduce-scatter.6.cloned.1.call-done = bf16[8,6144]{1,0:T(8,128)(2,1)} async-done(((bf16[32,6144]{1,0:T(8,128)(2,1)}), bf16[8,6144]{1,0:T(8,128)(2,1)}) %reduce-scatter.6.cloned.1.call-update) | async-done | bytes 98320 | tf_op jit(solution)/shard_map/reduce_scatter | solution.py:35
  337.0 2.0 reshape.166
  340.4 30.7 %all_to_all.82 = bf16[32,2,6144]{2,1,0:T(2,128)(2,1)} all-to-all(bf16[32,2,6144]{2,1,0:T(2,128)(2,1)S(1)} %bitcast.115), channel_id=1, replica_groups=mesh['seg'=8,'ep_0'=8,'ep_1'=4] {'ep_0','ep_1'}, dimensions={0} | all-to-all | bytes 1572864 | tf_op jit(solution)/shard_map/all_to_all | solution.py:156
  371.2 3.0 stack_reshape.2
  376.0 77.4 %all_to_all.83 = bf16[8,64,6144]{2,1,0:T(8,128)(2,1)} all-to-all(bf16[8,64,6144]{2,1,0:T(8,128)(2,1)S(1)} %stack.3), channel_id=1, replica_groups=mesh['seg'=8,'ep_0'=8,'ep_1'=4] {'seg'}, dimensions={0} | all-to-all | bytes 12582912 | tf_op jit(solution)/shard_map/all_to_all | solution.py:160
  453.4 12.0 %convolution_convert_fusion = bf16[512,6144]{1,0:T(8,128)(2,1)} fusion(bf16[1,288,6144]{2,1,0:T(8,128)(2,1)S(1)} %copy-done, bf16[512,6144]{1,0:T(8,128)(2,1)} %bitcast.110, bf16[1,6144,288]{1,2,0:T(8,128)(2,1)} %param.20), kind=kOutput, calls=%fused_computation.10 | convolution fusion | flops 3627761664 | bytes 19660800 | tf_op jit(solution)/shard_map/dot_general | solution.py:59
  465.4 2.5 all_to_all.68
  468.0 5.6 %all-to-all-start.3 = ((bf16[32,64,256]{2,1,0:T(8,128)(2,1)}), bf16[32,64,256]{2,1,0:T(8,128)(2,1)}, u32[]{:S(2)}, u32[]{:S(2)}) async-start(bf16[32,64,256]{2,1,0:T(8,128)(2,1)} %all_to_all.68), calls=%async_computation.3 | async-start | bytes 2097152 | tf_op jit(solution)/shard_map/all_to_all | solution.py:124
  473.7 27.7 %all-to-all-done.3 = bf16[32,64,256]{2,1,0:T(8,128)(2,1)} async-done(((bf16[32,64,256]{2,1,0:T(8,128)(2,1)}), bf16[32,64,256]{2,1,0:T(8,128)(2,1)}, u32[]{:S(2)}, u32[]{:S(2)}) %all-to-all-start.3) | async-done | bytes 1048608 | tf_op jit(solution)/shard_map/all_to_all | solution.py:124
  506.0 2.9 convert_element_type.93
  508.8 10.0 %all-to-all-start.7 = ((bf16[32,2,6144]{2,1,0:T(2,128)(2,1)}), bf16[32,2,6144]{2,1,0:T(2,128)(2,1)}, u32[]{:S(2)}, u32[]{:S(2)}) async-start(bf16[32,2,6144]{2,1,0:T(2,128)(2,1)} %convert_element_type.93), calls=%async_computation.10 | async-start | bytes 1572864 | tf_op jit(solution)/shard_map/all_to_all | solution.py:168
  518.8 2.8 multiply_convert_fusion.1
  521.7 18.8 %all-to-all-done.7 = bf16[32,2,6144]{2,1,0:T(2,128)(2,1)} async-done(((bf16[32,2,6144]{2,1,0:T(2,128)(2,1)}), bf16[32,2,6144]{2,1,0:T(2,128)(2,1)}, u32[]{:S(2)}, u32[]{:S(2)}) %all-to-all-start.7) | async-done | bytes 786464 | tf_op jit(solution)/shard_map/all_to_all | solution.py:168
  540.4 2.0 convert.7
  (97 shorter events, 64.0 us)
Async XLA Ops:
  7.2 446.2 %copy-start = (bf16[1,288,6144]{2,1,0:T(8,128)(2,1)S(1)}, bf16[1,288,6144]{2,1,0:T(8,128)(2,1)}, u32[]{:S(2)}) copy-start(bf16[1,288,6144]{2,1,0:T(8,128)(2,1)} %param.21) | copy-start | bytes 10616836
  9.7 46.3 %copy-start.4 = (f32[2048,2]{0,1:T(2,128)S(1)}, f32[2048,2]{0,1:T(2,128)}, u32[]{:S(2)}) copy-start(f32[2048,2]{0,1:T(2,128)} %param.15) | copy-start | bytes 49156
  9.7 39.9 %all-to-all-start.1 = ((bf16[64,32,256]{2,0,1:T(8,128)(2,1)}), bf16[64,32,256]{2,0,1:T(8,128)(2,1)}, u32[]{:S(2)}, u32[]{:S(2)}) async-start(bf16[64,32,256]{2,0,1:T(8,128)(2,1)} %bitcast.114), calls=%async_computation.1 | async-start | bytes 2097152 | tf_op jit(solution)/shard_map/all_to_all | solution.py:70
  49.6 32.7 %all-to-all-start.2 = ((bf16[64,32,256]{2,0,1:T(8,128)(2,1)}), bf16[64,32,256]{2,0,1:T(8,128)(2,1)}, u32[]{:S(2)}, u32[]{:S(2)}) async-start(bf16[64,32,256]{2,0,1:T(8,128)(2,1)} %bitcast.112), calls=%async_computation.2 | async-start | bytes 2097152 | tf_op jit(solution)/shard_map/all_to_all | solution.py:71
  55.2 209.8 %all-gather.2.cloned.1.call-start = ((), (), s32[]{:S(2)}) async-start(), calls=%async_computation.11 | async-start | bytes 3538944 | tf_op jit(solution)/shard_map/all_gather | solution.py:140
  82.3 40.3 %all-to-all-start = ((bf16[64,32,256]{2,0,1:T(8,128)(2,1)}), bf16[64,32,256]{2,0,1:T(8,128)(2,1)}, u32[]{:S(2)}, u32[]{:S(2)}) async-start(bf16[64,32,256]{2,0,1:T(8,128)(2,1)} %bitcast.113), calls=%async_computation | async-start | bytes 2097152 | tf_op jit(solution)/shard_map/all_to_all | solution.py:69
  99.6 18.7 %copy-start.1 = (bf16[2048,2,128]{2,1,0:T(2,128)(2,1)S(1)}, bf16[2048,2,128]{2,1,0:T(2,128)(2,1)}, u32[]{:S(2)}) copy-start(bf16[2048,2,128]{2,1,0:T(2,128)(2,1)} %reshape.161) | copy-start | bytes 3145732
  119.6 7.4 %copy-start.7 = (bf16[8,2,1]{0,1,2:T(2,128)(2,1)}, bf16[8,2,1]{0,1,2:T(2,128)(2,1)S(1)}, u32[]{:S(2)}) copy-start(bf16[8,2,1]{0,1,2:T(2,128)(2,1)S(1)} %copy.159) | copy-start | bytes 100
  226.5 6.7 %copy-start.3 = (f32[2048,2]{0,1:T(2,128)S(1)}, f32[2048,2]{0,1:T(2,128)}, u32[]{:S(2)}) copy-start(f32[2048,2]{0,1:T(2,128)} %get-tuple-element.131) | copy-start | bytes 49156
  244.2 0.7 copy-start.2
  245.6 18.5 %all-to-all-start.4 = ((f32[32,1,256]{2,1,0:T(1,128)}), f32[32,1,256]{2,1,0:T(1,128)}, u32[]{:S(2)}, u32[]{:S(2)}) async-start(f32[32,1,256]{2,1,0:T(1,128)} %broadcast_in_dim.85), calls=%async_computation.4 | async-start | bytes 65536 | tf_op jit(solution)/shard_map/all_to_all | solution.py:26
  255.5 56.2 %reduce-scatter.4.cloned.1.call-start = ((), (), s32[]{:S(2)}) async-start(), calls=%async_computation.12 | async-start | bytes 3538944 | tf_op jit(solution)/shard_map/reduce_scatter | solution.py:35
  269.7 42.3 %copy-start.5 = (s32[8,2]{0,1:T(2,128)S(1)}, s32[8,2]{0,1:T(2,128)}, u32[]{:S(2)}) copy-start(s32[8,2]{0,1:T(2,128)} %param.18) | copy-start | bytes 196
  269.7 65.3 %reduce-scatter.6.cloned.1.call-start = ((), (), s32[]{:S(2)}) async-start(), calls=%async_computation.13 | async-start | bytes 491520 | tf_op jit(solution)/shard_map/reduce_scatter | solution.py:35
  311.7 194.3 %reduce-scatter.8.cloned.1.call-start = ((), (), s32[]{:S(2)}) async-start(), calls=%async_computation.14 | async-start | bytes 7077888 | tf_op jit(solution)/shard_map/reduce_scatter | solution.py:162
  465.4 8.2 %copy-start.6 = (f32[8,2]{0,1:T(2,128)S(1)}, f32[8,2]{0,1:T(2,128)}, u32[]{:S(2)}) copy-start(f32[8,2]{0,1:T(2,128)} %param.19) | copy-start | bytes 196
  468.0 33.4 %all-to-all-start.3 = ((bf16[32,64,256]{2,1,0:T(8,128)(2,1)}), bf16[32,64,256]{2,1,0:T(8,128)(2,1)}, u32[]{:S(2)}, u32[]{:S(2)}) async-start(bf16[32,64,256]{2,1,0:T(8,128)(2,1)} %all_to_all.68), calls=%async_computation.3 | async-start | bytes 2097152 | tf_op jit(solution)/shard_map/all_to_all | solution.py:124
  508.8 31.6 %all-to-all-start.7 = ((bf16[32,2,6144]{2,1,0:T(2,128)(2,1)}), bf16[32,2,6144]{2,1,0:T(2,128)(2,1)}, u32[]{:S(2)}, u32[]{:S(2)}) async-start(bf16[32,2,6144]{2,1,0:T(2,128)(2,1)} %convert_element_type.93), calls=%async_computation.10 | async-start | bytes 1572864 | tf_op jit(solution)/shard_map/all_to_all | solution.py:168
Sparse Core Ops, SparseCore 0:
  57.9 31.4 all-gather.1
  269.8 41.8 reduce-scatter.3
  314.2 20.7 reduce-scatter.5
  465.6 40.2 reduce-scatter.7
